TPU v7x, 512 devices: a whole 4x8x8 slice. The times are simulated.
512 devices in a mesh: wide: 32 (over y, z_hi, core), grp: 16 (over x, z_lo).
Axes of the slice: x: 4, y: 8, z: 8 (z_hi: 2, z_lo: 4; z = z_hi * 4 + z_lo), core: 2. Of those that a mesh axis runs over, the one named last changes fastest.
Arguments:
- obs_value: float32 [65536], P(('wide', 'grp')), may hold values from -6 to 6
- obs_tile: int32 [65536], P(('wide', 'grp')), may hold values from 0 to 31
- obs_cell: int32 [65536], P(('wide', 'grp')), may hold values from 0 to 32767
- obs_type: int32 [65536], P(('wide', 'grp')), may hold values from 0 to 2
- obs_weights: float32 [2, 8], replicated, may hold values from 0.2 to 1.5
- diffusivity: float32 [128, 8192], P('wide', 'grp'), may hold values from 0.03 to 0.24
- erodibility: float32 [128, 8192], P('wide', 'grp'), may hold values from 0.1 to 1
- class_mixing: float32 [8, 8], replicated, may hold values from -2.5 to 2.5
- fall_table: float32 [16], replicated, may hold values from 0.05 to 0.6
- fall_index: int32 [8], replicated, may hold values from 0 to 15
- bedload_rate: float32 [8], replicated, may hold values from 20 to 3000
Outputs:
- adjoint_tracer: float32 [8, 16, 128, 8192], P(None, None, 'wide', 'grp')
- adjoint_bed: float32 [8, 128, 8192], P(None, 'wide', 'grp')
All inputs are finite; a program needn't handle non-finite values.
Results may differ from a plain program's by a relative error of at most 0.00019.
Values sent between devices are 32-bit elements; how exact they have to be, the bound alone decides.
No kernel may reach another device: no remote copies, remote signals or barrier semaphores. Data moves between devices by JAX's collectives and lax.ppermute only.
A program may use at most 64 MiB of HBM per device.

v0:
```python
import jax
import jax.numpy as jnp
from jax import lax
from jax.sharding import PartitionSpec as P

K = 16
STEPS = 2


def padded_2(array, sides, width):
    for axis, dim in sides:
        peers, length = (lax.axis_size(axis), array.shape[dim])
        up = [(i, (i + 1) % peers) for i in range(peers - 1)]
        down = [(j, i) for i, j in up]
        last = lax.slice_in_dim(array, length - width, length, axis=dim)
        first = lax.slice_in_dim(array, 0, width, axis=dim)
        before = lax.ppermute(last, axis, up)
        after = lax.ppermute(first, axis, down)
        array = jnp.concatenate([before, array, after], axis=dim)
    return array


def link(earlier, later):
    return (earlier[0] * later[0], later[0] * earlier[1] + later[1])


def local_sweep(rows, rate_rows):
    gain_f = 1.0 / (1.0 + rate_rows)
    gain_g = rate_rows / (1.0 + rate_rows)
    flipped = rows[:, ::-1]
    coeff = jnp.broadcast_to(gain_g[:, None], flipped.shape)
    return lax.associative_scan(link, (coeff, gain_f[:, None] * flipped), axis=1)


def local(
    obs_value,
    obs_tile,
    obs_cell,
    obs_type,
    obs_weights,
    diffusivity,
    erodibility,
    class_mixing,
    fall_table,
    fall_index,
    bedload_rate,
):
    classes = obs_weights.shape[1]
    tile_x, tile_y = diffusivity.shape
    cells = K * tile_x * tile_y
    values, tiles, places, kinds = (
        lax.all_gather(obs_value, "wide", axis=0, tiled=True),
        lax.all_gather(obs_tile, "wide", axis=0, tiled=True),
        lax.all_gather(obs_cell, "wide", axis=0, tiled=True),
        lax.all_gather(obs_type, "wide", axis=0, tiled=True),
    )
    mine = jnp.logical_and(kinds < 2, tiles == lax.axis_index("wide"))
    live = jnp.where(mine, values, 0.0)
    kind = jnp.where(kinds < 2, kinds, 0)
    fields = jnp.zeros((2, cells), jnp.float32).at[kind, places].add(live)
    fields = fields.reshape(2, K, tile_x, tile_y)
    lq = jnp.einsum("tc,tkxy->ckxy", obs_weights, fields, precision=lax.Precision.HIGHEST)
    lb = jnp.zeros((classes, tile_x, tile_y), jnp.float32)
    table_hit = fall_index[:, None] == jnp.arange(fall_table.shape[0], dtype=jnp.int32)[None, :]
    settle = jnp.sum(jnp.where(table_hit, fall_table[None, :], 0.0), axis=1)
    rate_rows = jnp.repeat(bedload_rate, tile_x)
    for step in range(STEPS):
        lb = lb + erodibility * jnp.einsum(
            "cd,cxy->dxy", class_mixing, lq[:, 0], precision=lax.Precision.HIGHEST
        )
        rows = lb.reshape(classes * tile_x, tile_y)
        moved = lax.all_to_all(rows, "grp", split_axis=0, concat_axis=1, tiled=True)
        share = moved.shape[0]
        my_rates = lax.dynamic_slice_in_dim(rate_rows, lax.axis_index("grp") * share, share)
        swept = local_sweep(moved, my_rates)
        solved = swept[1][:, ::-1]
        rows = lax.all_to_all(solved, "grp", split_axis=1, concat_axis=0, tiled=True)
        lb = rows.reshape(classes, tile_x, tile_y)
        lq = lq.at[:, 0].add(settle[:, None, None] * lb)
        below = jnp.concatenate([jnp.zeros_like(lq[:, :1]), lq[:, :-1]], axis=1)
        lq = (1.0 - settle)[:, None, None, None] * lq + settle[:, None, None, None] * below
        moment = diffusivity * lq
        padded = padded_2(moment, (("wide", 2), ("grp", 3)), 1)
        beside = (
            padded[:, :, 2:, 1:-1]
            + padded[:, :, :-2, 1:-1]
            + padded[:, :, 1:-1, 2:]
            + padded[:, :, 1:-1, :-2]
        )
        lq = lq - 4.0 * moment + beside
    return (lq, lb)


def solution(mesh):
    in_specs = (
        P(("wide", "grp")),
        P(("wide", "grp")),
        P(("wide", "grp")),
        P(("wide", "grp")),
        P(),
        P("wide", "grp"),
        P("wide", "grp"),
        P(),
        P(),
        P(),
        P(),
    )
    out_specs = (P(None, None, "wide", "grp"), P(None, "wide", "grp"))
    return jax.shard_map(local, mesh=mesh, in_specs=in_specs, out_specs=out_specs, check_vma=False)
```

profile of v0, /device:TPU:5, one launch (start us, length us, event | category | flops | bytes accessed | tf_op | source)
XLA Modules:
  0.0 467.2 jit_solution(3767252619659113177)
XLA Ops:
  1.3 58.4 %all-gather.3 = f32[32,1,128]{2,1,0:T(1,128)S(1)} all-gather(f32[1,1,128]{2,1,0:T(1,128)S(1)} %bitcast.94), channel_id=1, replica_groups=mesh['wide'=32,'grp'=16] {'wide'}, dimensions={0}, use_global_device_ids=true | all-gather | bytes 16896 | tf_op jit(solution)/shard_map/all_gather | solution.py:52
  60.4 46.3 %all-gather.2 = s32[32,1,128]{2,1,0:T(1,128)S(1)} all-gather(s32[1,1,128]{2,1,0:T(1,128)S(1)} %bitcast.95), channel_id=1, replica_groups=mesh['wide'=32,'grp'=16] {'wide'}, dimensions={0}, use_global_device_ids=true | all-gather | bytes 16896 | tf_op jit(solution)/shard_map/all_gather | solution.py:53
  107.4 51.6 %all-gather.1 = s32[32,1,128]{2,1,0:T(1,128)S(1)} all-gather(s32[1,1,128]{2,1,0:T(1,128)S(1)} %bitcast.96), channel_id=1, replica_groups=mesh['wide'=32,'grp'=16] {'wide'}, dimensions={0}, use_global_device_ids=true | all-gather | bytes 16896 | tf_op jit(solution)/shard_map/all_gather | solution.py:54
  159.6 46.3 %all-gather = s32[32,1,128]{2,1,0:T(1,128)S(1)} all-gather(s32[1,1,128]{2,1,0:T(1,128)S(1)} %bitcast.97), channel_id=1, replica_groups=mesh['wide'=32,'grp'=16] {'wide'}, dimensions={0}, use_global_device_ids=true | all-gather | bytes 16896 | tf_op jit(solution)/shard_map/all_gather | solution.py:55
  207.4 22.0 %scatter_custom_fusion = f32[65536]{0:T(1024)S(1)} fusion(s32[4096]{0:T(1024)S(1)} %broadcast_select_fusion, f32[4096]{0:T(1024)S(1)} %fusion.25, f32[]{:T(128)} %constant.65.clone.1), kind=kCustom, calls=%fused_computation.42 | custom fusion | flops 4096 | bytes 262148
  232.3 7.0 %all-to-all-start = ((f32[16,2,512]{2,1,0:T(2,128)}), f32[16,2,512]{2,1,0:T(2,128)S(1)}, u32[]{:S(2)}, u32[]{:S(2)}) async-start(f32[16,2,512]{2,1,0:T(2,128)} %all_to_all.52), calls=%async_computation | async-start | bytes 131072 | tf_op jit(solution)/shard_map/all_to_all | solution.py:72
  241.3 3.3 all-to-all-done
  244.6 5.6 %rev.12 = f32[2,8192]{1,0:T(2,128)S(1)} reverse(f32[2,8192]{1,0:T(2,128)S(1)} %bitcast.71), dimensions={1} | reverse | bytes 131072 | tf_op jit(solution)/shard_map/rev | solution.py:30
  277.5 20.6 %rev.13 = f32[2,8192]{1,0:T(2,128)} reverse(f32[2,8192]{1,0:T(2,128)S(1)} %add.446), dimensions={1} | reverse | bytes 131072 | tf_op jit(solution)/shard_map/rev | solution.py:76
  298.1 5.0 %all-to-all-start.1 = ((f32[2,16,512]{2,0,1:T(2,128)}), f32[2,16,512]{2,0,1:T(2,128)S(1)}, u32[]{:S(2)}, u32[]{:S(2)}) async-start(f32[2,16,512]{2,0,1:T(2,128)} %bitcast.22), calls=%async_computation.1 | async-start | bytes 131072 | tf_op jit(solution)/shard_map/all_to_all | solution.py:77
  303.2 5.1 %all-to-all-done.1 = f32[2,16,512]{2,0,1:T(2,128)S(1)} async-done(((f32[2,16,512]{2,0,1:T(2,128)}), f32[2,16,512]{2,0,1:T(2,128)S(1)}, u32[]{:S(2)}, u32[]{:S(2)}) %all-to-all-start.1) | async-done | bytes 65568 | tf_op jit(solution)/shard_map/all_to_all | solution.py:77
  310.1 9.9 %collective-permute-start.1 = (f32[8,16,1,512]{3,0,2,1:T(8,128)S(1)}, f32[8,16,1,512]{3,0,2,1:T(8,128)S(1)}, u32[]{:S(2)}, u32[]{:S(2)}) collective-permute-start(f32[8,16,1,512]{3,0,2,1:T(8,128)S(1)} %get-tuple-element.47), channel_id=1, source_target_pairs={{0,16},{16,32},{32,48},{48,64},{64,80},{80,96},{96,112},{112,128},... | collective-permute-start | bytes 786440 | tf_op jit(solution)/shard_map/ppermute | solution.py:17
  321.9 10.1 %collective-permute-done.1 = f32[8,16,1,512]{3,0,2,1:T(8,128)S(1)} collective-permute-done((f32[8,16,1,512]{3,0,2,1:T(8,128)S(1)}, f32[8,16,1,512]{3,0,2,1:T(8,128)S(1)}, u32[]{:S(2)}, u32[]{:S(2)}) %collective-permute-start.1) | collective-permute-done | bytes 262176 | tf_op jit(solution)/shard_map/ppermute | solution.py:17
  334.2 3.5 collective-permute-start.2
  339.7 9.3 %collective-permute-done.2 = f32[8,16,6,1]{3,0,2,1:T(8,128)S(1)} collective-permute-done((f32[8,16,6,1]{3,0,2,1:T(8,128)}, f32[8,16,6,1]{3,0,2,1:T(8,128)S(1)}, u32[]{:S(2)}, u32[]{:S(2)}) %collective-permute-start.2) | collective-permute-done | bytes 3104 | tf_op jit(solution)/shard_map/ppermute | solution.py:18
  352.5 10.3 %all_to_all.70 = f32[16,2,512]{2,1,0:T(2,128)S(1)} all-to-all(f32[16,2,512]{2,1,0:T(2,128)S(1)} %all_to_all.59), channel_id=1, replica_groups=mesh['wide'=32,'grp'=16] {'grp'}, dimensions={0} | all-to-all | bytes 131072 | tf_op jit(solution)/shard_map/all_to_all | solution.py:72
  362.8 5.6 %rev.14 = f32[2,8192]{1,0:T(2,128)S(1)} reverse(f32[2,8192]{1,0:T(2,128)S(1)} %bitcast.72), dimensions={1} | reverse | bytes 131072 | tf_op jit(solution)/shard_map/rev | solution.py:30
  401.6 5.6 %rev.15 = f32[2,8192]{1,0:T(2,128)S(1)} reverse(f32[2,8192]{1,0:T(2,128)S(1)} %add.491), dimensions={1} | reverse | bytes 131072 | tf_op jit(solution)/shard_map/rev | solution.py:76
  407.1 9.6 %all_to_all.71 = f32[2,16,512]{2,0,1:T(2,128)S(1)} all-to-all(f32[2,16,512]{2,0,1:T(2,128)S(1)} %bitcast.73), channel_id=1, replica_groups=mesh['wide'=32,'grp'=16] {'grp'}, dimensions={1} | all-to-all | bytes 131072 | tf_op jit(solution)/shard_map/all_to_all | solution.py:77
  418.4 13.4 %collective-permute-start.5 = (f32[8,16,1,512]{3,0,2,1:T(8,128)S(1)}, f32[8,16,1,512]{3,0,2,1:T(8,128)S(1)}, u32[]{:S(2)}, u32[]{:S(2)}) collective-permute-start(f32[8,16,1,512]{3,0,2,1:T(8,128)S(1)} %get-tuple-element.45), channel_id=1, source_target_pairs={{0,16},{16,32},{32,48},{48,64},{64,80},{80,96},{96,112},{112,128},... | collective-permute-start | bytes 786440 | tf_op jit(solution)/shard_map/ppermute | solution.py:17
  433.7 7.6 %collective-permute-done.5 = f32[8,16,1,512]{3,0,2,1:T(8,128)S(1)} collective-permute-done((f32[8,16,1,512]{3,0,2,1:T(8,128)S(1)}, f32[8,16,1,512]{3,0,2,1:T(8,128)S(1)}, u32[]{:S(2)}, u32[]{:S(2)}) %collective-permute-start.5) | collective-permute-done | bytes 262176 | tf_op jit(solution)/shard_map/ppermute | solution.py:17
  444.5 4.1 collective-permute-start.6
  451.8 4.8 %collective-permute-done.6 = f32[8,16,6,1]{3,0,2,1:T(8,128)} collective-permute-done((f32[8,16,6,1]{3,0,2,1:T(8,128)}, f32[8,16,6,1]{3,0,2,1:T(8,128)}, u32[]{:S(2)}, u32[]{:S(2)}) %collective-permute-start.6) | collective-permute-done | bytes 3104 | tf_op jit(solution)/shard_map/ppermute | solution.py:18
  456.6 6.6 %collective-permute-done.7 = f32[8,16,6,1]{3,0,2,1:T(8,128)} collective-permute-done((f32[8,16,6,1]{3,0,2,1:T(8,128)}, f32[8,16,6,1]{3,0,2,1:T(8,128)}, u32[]{:S(2)}, u32[]{:S(2)}) %collective-permute-start.7) | collective-permute-done | bytes 3104 | tf_op jit(solution)/shard_map/ppermute | solution.py:17
  (416 shorter events, 93.4 us)
Async XLA Ops:
  0.6 230.6 %copy-start = (f32[8,8]{1,0:T(8,128)S(1)}, f32[8,8]{1,0:T(8,128)}, u32[]{:S(2)}) copy-start(f32[8,8]{1,0:T(8,128)} %param.22) | copy-start | bytes 772
  232.3 12.4 %all-to-all-start = ((f32[16,2,512]{2,1,0:T(2,128)}), f32[16,2,512]{2,1,0:T(2,128)S(1)}, u32[]{:S(2)}, u32[]{:S(2)}) async-start(f32[16,2,512]{2,1,0:T(2,128)} %all_to_all.52), calls=%async_computation | async-start | bytes 131072 | tf_op jit(solution)/shard_map/all_to_all | solution.py:72
  240.2 22.6 %copy-start.46 = (f32[2]{0:T(128)}, f32[2]{0:T(128)S(1)}, u32[]{:S(2)}) copy-start(f32[2]{0:T(128)S(1)} %get-tuple-element.37) | copy-start | bytes 28
  240.2 24.3 %copy-start.22 = (f32[2]{0:T(128)}, f32[2]{0:T(128)S(1)}, u32[]{:S(2)}) copy-start(f32[2]{0:T(128)S(1)} %get-tuple-element.38) | copy-start | bytes 28
  240.2 27.5 %copy-start.20 = (f32[2]{0:T(128)}, f32[2]{0:T(128)S(1)}, u32[]{:S(2)}) copy-start(f32[2]{0:T(128)S(1)} %get-tuple-element.39) | copy-start | bytes 28
  240.2 24.7 %copy-start.32 = (f32[2]{0:T(128)}, f32[2]{0:T(128)S(1)}, u32[]{:S(2)}) copy-start(f32[2]{0:T(128)S(1)} %get-tuple-element.68) | copy-start | bytes 28
  240.2 25.2 %copy-start.30 = (f32[2]{0:T(128)}, f32[2]{0:T(128)S(1)}, u32[]{:S(2)}) copy-start(f32[2]{0:T(128)S(1)} %get-tuple-element.66) | copy-start | bytes 28
  240.2 26.2 %copy-start.40 = (f32[2]{0:T(128)}, f32[2]{0:T(128)S(1)}, u32[]{:S(2)}) copy-start(f32[2]{0:T(128)S(1)} %get-tuple-element.67) | copy-start | bytes 28
  240.2 28.7 %copy-start.28 = (f32[2]{0:T(128)}, f32[2]{0:T(128)S(1)}, u32[]{:S(2)}) copy-start(f32[2]{0:T(128)S(1)} %get-tuple-element.61) | copy-start | bytes 28
  240.2 30.4 %copy-start.26 = (f32[2]{0:T(128)}, f32[2]{0:T(128)S(1)}, u32[]{:S(2)}) copy-start(f32[2]{0:T(128)S(1)} %get-tuple-element.62) | copy-start | bytes 28
  240.3 23.1 %copy-start.38 = (f32[2]{0:T(128)}, f32[2]{0:T(128)S(1)}, u32[]{:S(2)}) copy-start(f32[2]{0:T(128)S(1)} %get-tuple-element.57) | copy-start | bytes 28
  240.3 23.5 %copy-start.36 = (f32[2]{0:T(128)}, f32[2]{0:T(128)S(1)}, u32[]{:S(2)}) copy-start(f32[2]{0:T(128)S(1)} %get-tuple-element.63) | copy-start | bytes 28
  240.3 23.8 %copy-start.34 = (f32[2]{0:T(128)}, f32[2]{0:T(128)S(1)}, u32[]{:S(2)}) copy-start(f32[2]{0:T(128)S(1)} %get-tuple-element.58) | copy-start | bytes 28
  240.5 22.3 %copy-start.48 = (f32[2,1]{1,0:T(2,128)}, f32[2,1]{1,0:T(2,128)S(1)}, u32[]{:S(2)}) copy-start(f32[2,1]{1,0:T(2,128)S(1)} %copy.64) | copy-start | bytes 28
  241.3 67.2 %copy-start.24 = (f32[8]{0:T(128)}, f32[8]{0:T(128)S(1)}, u32[]{:S(2)}) copy-start(f32[8]{0:T(128)S(1)} %select_reduce_fusion) | copy-start | bytes 100
  298.1 10.2 %all-to-all-start.1 = ((f32[2,16,512]{2,0,1:T(2,128)}), f32[2,16,512]{2,0,1:T(2,128)S(1)}, u32[]{:S(2)}, u32[]{:S(2)}) async-start(f32[2,16,512]{2,0,1:T(2,128)} %bitcast.22), calls=%async_computation.1 | async-start | bytes 131072 | tf_op jit(solution)/shard_map/all_to_all | solution.py:77
  310.1 21.8 %collective-permute-start.1 = (f32[8,16,1,512]{3,0,2,1:T(8,128)S(1)}, f32[8,16,1,512]{3,0,2,1:T(8,128)S(1)}, u32[]{:S(2)}, u32[]{:S(2)}) collective-permute-start(f32[8,16,1,512]{3,0,2,1:T(8,128)S(1)} %get-tuple-element.47), channel_id=1, source_target_pairs={{0,16},{16,32},{32,48},{48,64},{64,80},{80,96},{96,112},{112,128},... | collective-permute-start | bytes 786440 | tf_op jit(solution)/shard_map/ppermute | solution.py:17
  320.0 13.3 %collective-permute-start = (f32[8,16,1,512]{3,0,2,1:T(8,128)S(1)}, f32[8,16,1,512]{3,0,2,1:T(8,128)S(1)}, u32[]{:S(2)}, u32[]{:S(2)}) collective-permute-start(f32[8,16,1,512]{3,0,2,1:T(8,128)S(1)} %get-tuple-element.48), channel_id=1, source_target_pairs={{16,0},{32,16},{48,32},{64,48},{80,64},{96,80},{112,96},{128,112},... | collective-permute-start | bytes 786440 | tf_op jit(solution)/shard_map/ppermute | solution.py:18
  334.2 14.8 %collective-permute-start.2 = (f32[8,16,6,1]{3,0,2,1:T(8,128)}, f32[8,16,6,1]{3,0,2,1:T(8,128)S(1)}, u32[]{:S(2)}, u32[]{:S(2)}) collective-permute-start(f32[8,16,6,1]{3,0,2,1:T(8,128)} %get-tuple-element.43), channel_id=1, source_target_pairs={{1,0},{2,1},{3,2},{4,3},{5,4},{6,5},{7,6},{8,7},{9,8},{10,9},{11,1... | collective-permute-start | bytes 9224 | tf_op jit(solution)/shard_map/ppermute | solution.py:18
  337.7 12.1 %collective-permute-start.3 = (f32[8,16,6,1]{3,0,2,1:T(8,128)S(1)}, f32[8,16,6,1]{3,0,2,1:T(8,128)}, u32[]{:S(2)}, u32[]{:S(2)}) collective-permute-start(f32[8,16,6,1]{3,0,2,1:T(8,128)S(1)} %get-tuple-element.44), channel_id=1, source_target_pairs={{0,1},{1,2},{2,3},{3,4},{4,5},{5,6},{6,7},{7,8},{8,9},{9,10},{10,1... | collective-permute-start | bytes 9224 | tf_op jit(solution)/shard_map/ppermute | solution.py:17
  418.4 22.9 %collective-permute-start.5 = (f32[8,16,1,512]{3,0,2,1:T(8,128)S(1)}, f32[8,16,1,512]{3,0,2,1:T(8,128)S(1)}, u32[]{:S(2)}, u32[]{:S(2)}) collective-permute-start(f32[8,16,1,512]{3,0,2,1:T(8,128)S(1)} %get-tuple-element.45), channel_id=1, source_target_pairs={{0,16},{16,32},{32,48},{48,64},{64,80},{80,96},{96,112},{112,128},... | collective-permute-start | bytes 786440 | tf_op jit(solution)/shard_map/ppermute | solution.py:17
  431.7 11.7 %collective-permute-start.4 = (f32[8,16,1,512]{3,0,2,1:T(8,128)S(1)}, f32[8,16,1,512]{3,0,2,1:T(8,128)S(1)}, u32[]{:S(2)}, u32[]{:S(2)}) collective-permute-start(f32[8,16,1,512]{3,0,2,1:T(8,128)S(1)} %get-tuple-element.46), channel_id=1, source_target_pairs={{16,0},{32,16},{48,32},{64,48},{80,64},{96,80},{112,96},{128,112},... | collective-permute-start | bytes 786440 | tf_op jit(solution)/shard_map/ppermute | solution.py:18
  444.5 12.1 %collective-permute-start.6 = (f32[8,16,6,1]{3,0,2,1:T(8,128)}, f32[8,16,6,1]{3,0,2,1:T(8,128)}, u32[]{:S(2)}, u32[]{:S(2)}) collective-permute-start(f32[8,16,6,1]{3,0,2,1:T(8,128)} %get-tuple-element.41), channel_id=1, source_target_pairs={{1,0},{2,1},{3,2},{4,3},{5,4},{6,5},{7,6},{8,7},{9,8},{10,9},{11,1... | collective-permute-start | bytes 9224 | tf_op jit(solution)/shard_map/ppermute | solution.py:18
  448.6 14.6 %collective-permute-start.7 = (f32[8,16,6,1]{3,0,2,1:T(8,128)}, f32[8,16,6,1]{3,0,2,1:T(8,128)}, u32[]{:S(2)}, u32[]{:S(2)}) collective-permute-start(f32[8,16,6,1]{3,0,2,1:T(8,128)} %get-tuple-element.42), channel_id=1, source_target_pairs={{0,1},{1,2},{2,3},{3,4},{4,5},{5,6},{6,7},{7,8},{8,9},{9,10},{10,1... | collective-permute-start | bytes 9224 | tf_op jit(solution)/shard_map/ppermute | solution.py:17
  (60 other events, 98.6 us)
where the time goes:
time: 474 us; the launch traced here: 467 us
  blocking collectives  223 us (47%)
  local copies, waits for them, and re-layouts  104 us (22%)
  starting transfers between devices  51.1 us (11%)
  waiting for transfers between devices  50.3 us (11%)
  other arithmetic  35.5 us (7%)
    all_gather x1, blocking collectives, local(): lax.all_gather(obs_value, 'wide', axis=0, tiled=True)  58.4 us
    all_gather x1, blocking collectives, local(): lax.all_gather(obs_cell, 'wide', axis=0, tiled=True)  51.6 us
    all_gather x1, blocking collectives, local(): lax.all_gather(obs_tile, 'wide', axis=0, tiled=True)  46.3 us
    all_gather x1, blocking collectives, local(): lax.all_gather(obs_type, 'wide', axis=0, tiled=True)  46.3 us
    slice x94, local copies, waits for them, and re-layouts, local_sweep(): lax.associative_scan(link, (coeff, gain_f[:, None] * flipped), axis=1)  29.3 us
    ppermute x4, starting transfers between devices, padded_2(): before = lax.ppermute(last, axis, up)  27.6 us
    rev x2, local copies, waits for them, and re-layouts, local(): solved = swept[1][:, ::-1]  26.2 us
    ppermute x4, waiting for transfers between devices, padded_2(): before = lax.ppermute(last, axis, up)  24.3 us
  transfers between devices with their start and end apart: 10, of which 9 were waited for; matrix products, arithmetic and copies ran while one was open for 0% of the time, Pallas kernels for 0%

commit v1 on v0

--- a/solution.py
+++ b/solution.py
@@ -49,7 +49,9 @@
     tile_x, tile_y = diffusivity.shape
     cells = K * tile_x * tile_y
     values, tiles, places, kinds = (
-        lax.all_gather(obs_value, "wide", axis=0, tiled=True),
+        jnp.concatenate(
+            lax.all_to_all(jnp.stack([obs_value] * lax.axis_size("wide")), "wide", 0, 0), axis=0
+        ),
         lax.all_gather(obs_tile, "wide", axis=0, tiled=True),
         lax.all_gather(obs_cell, "wide", axis=0, tiled=True),
         lax.all_gather(obs_type, "wide", axis=0, tiled=True),

time: 474 us -> 442 us (0.932)
  the two profiles are of different devices: /device:TPU:5 before, /device:TPU:35 now
where the time goes in v1:
time: 442 us; the launch traced here: 435 us
  blocking collectives  170 us (38%)
  local copies, waits for them, and re-layouts  104 us (24%)
  waiting for transfers between devices  62.3 us (14%)
  starting transfers between devices  59.2 us (13%)
  other arithmetic  35.5 us (8%)
    all_gather x1, blocking collectives, local(): lax.all_gather(obs_cell, 'wide', axis=0, tiled=True)  51.6 us
    all_gather x1, blocking collectives, local(): lax.all_gather(obs_tile, 'wide', axis=0, tiled=True)  51.4 us
    all_gather x1, blocking collectives, local(): lax.all_gather(obs_type, 'wide', axis=0, tiled=True)  46.6 us
    slice x94, local copies, waits for them, and re-layouts, local_sweep(): lax.associative_scan(link, (coeff, gain_f[:, None] * flipped), axis=1)  29.3 us
    ppermute x4, waiting for transfers between devices, padded_2(): after = lax.ppermute(first, axis, down)  29.1 us
    rev x2, local copies, waits for them, and re-layouts, local(): solved = swept[1][:, ::-1]  26.2 us
    ppermute x4, waiting for transfers between devices, padded_2(): before = lax.ppermute(last, axis, up)  22.3 us
    unnamed x4, other arithmetic  22.2 us
  transfers between devices with their start and end apart: 11, of which 10 were waited for; matrix products, arithmetic and copies ran while one was open for 0% of the time, Pallas kernels for 0%

profile of v1, /device:TPU:35, one launch (start us, length us, event | category | flops | bytes accessed | tf_op | source)
XLA Modules:
  0.0 435.3 jit_solution(8111914809673998528)
XLA Ops:
  1.9 16.1 %all-to-all-start = ((f32[32,1,128]{2,1,0:T(1,128)}), f32[32,1,128]{2,1,0:T(1,128)S(1)}, u32[]{:S(2)}, u32[]{:S(2)}) async-start(f32[32,1,128]{2,1,0:T(1,128)} %stack.2), calls=%async_computation | async-start | bytes 32768 | tf_op jit(solution)/shard_map/all_to_all | solution.py:53
  19.5 51.6 %all-gather.1 = s32[32,1,128]{2,1,0:T(1,128)S(1)} all-gather(s32[1,1,128]{2,1,0:T(1,128)S(1)} %bitcast.93), channel_id=1, replica_groups=mesh['wide'=32,'grp'=16] {'wide'}, dimensions={0}, use_global_device_ids=true | all-gather | bytes 16896 | tf_op jit(solution)/shard_map/all_gather | solution.py:56
  71.8 46.6 %all-gather = s32[32,1,128]{2,1,0:T(1,128)S(1)} all-gather(s32[1,1,128]{2,1,0:T(1,128)S(1)} %bitcast.94), channel_id=1, replica_groups=mesh['wide'=32,'grp'=16] {'wide'}, dimensions={0}, use_global_device_ids=true | all-gather | bytes 16896 | tf_op jit(solution)/shard_map/all_gather | solution.py:57
  120.6 51.4 %all-gather.2 = s32[32,1,128]{2,1,0:T(1,128)S(1)} all-gather(s32[1,1,128]{2,1,0:T(1,128)S(1)} %bitcast.95), channel_id=1, replica_groups=mesh['wide'=32,'grp'=16] {'wide'}, dimensions={0}, use_global_device_ids=true | all-gather | bytes 16896 | tf_op jit(solution)/shard_map/all_gather | solution.py:55
  172.0 22.0 %scatter_custom_fusion = f32[65536]{0:T(1024)S(1)} fusion(s32[4096]{0:T(1024)S(1)} %broadcast_select_fusion, f32[4096]{0:T(1024)S(1)} %fusion.25, f32[]{:T(128)} %constant.65.clone.1), kind=kCustom, calls=%fused_computation.42 | custom fusion | flops 4096 | bytes 262148
  196.8 7.0 %all-to-all-start.1 = ((f32[16,2,512]{2,1,0:T(2,128)}), f32[16,2,512]{2,1,0:T(2,128)S(1)}, u32[]{:S(2)}, u32[]{:S(2)}) async-start(f32[16,2,512]{2,1,0:T(2,128)} %all_to_all.57), calls=%async_computation.1 | async-start | bytes 131072 | tf_op jit(solution)/shard_map/all_to_all | solution.py:74
  204.9 4.9 %all-to-all-done.1 = f32[16,2,512]{2,1,0:T(2,128)S(1)} async-done(((f32[16,2,512]{2,1,0:T(2,128)}), f32[16,2,512]{2,1,0:T(2,128)S(1)}, u32[]{:S(2)}, u32[]{:S(2)}) %all-to-all-start.1) | async-done | bytes 65568 | tf_op jit(solution)/shard_map/all_to_all | solution.py:74
  209.8 5.6 %rev.12 = f32[2,8192]{1,0:T(2,128)S(1)} reverse(f32[2,8192]{1,0:T(2,128)S(1)} %bitcast.70), dimensions={1} | reverse | bytes 131072 | tf_op jit(solution)/shard_map/rev | solution.py:30
  242.6 20.6 %rev.13 = f32[2,8192]{1,0:T(2,128)} reverse(f32[2,8192]{1,0:T(2,128)S(1)} %add.446), dimensions={1} | reverse | bytes 131072 | tf_op jit(solution)/shard_map/rev | solution.py:78
  263.3 4.5 %all-to-all-start.2 = ((f32[2,16,512]{2,0,1:T(2,128)}), f32[2,16,512]{2,0,1:T(2,128)S(1)}, u32[]{:S(2)}, u32[]{:S(2)}) async-start(f32[2,16,512]{2,0,1:T(2,128)} %bitcast.21), calls=%async_computation.2 | async-start | bytes 131072 | tf_op jit(solution)/shard_map/all_to_all | solution.py:79
  267.9 5.9 %all-to-all-done.2 = f32[2,16,512]{2,0,1:T(2,128)S(1)} async-done(((f32[2,16,512]{2,0,1:T(2,128)}), f32[2,16,512]{2,0,1:T(2,128)S(1)}, u32[]{:S(2)}, u32[]{:S(2)}) %all-to-all-start.2) | async-done | bytes 65568 | tf_op jit(solution)/shard_map/all_to_all | solution.py:79
  275.5 4.8 %collective-permute-start.1 = (f32[8,16,1,512]{3,0,2,1:T(8,128)S(1)}, f32[8,16,1,512]{3,0,2,1:T(8,128)S(1)}, u32[]{:S(2)}, u32[]{:S(2)}) collective-permute-start(f32[8,16,1,512]{3,0,2,1:T(8,128)S(1)} %get-tuple-element.47), channel_id=1, source_target_pairs={{0,16},{16,32},{32,48},{48,64},{64,80},{80,96},{96,112},{112,128},... | collective-permute-start | bytes 786440 | tf_op jit(solution)/shard_map/ppermute | solution.py:17
  283.7 14.4 %collective-permute-done = f32[8,16,1,512]{3,0,2,1:T(8,128)S(1)} collective-permute-done((f32[8,16,1,512]{3,0,2,1:T(8,128)S(1)}, f32[8,16,1,512]{3,0,2,1:T(8,128)S(1)}, u32[]{:S(2)}, u32[]{:S(2)}) %collective-permute-start) | collective-permute-done | bytes 262176 | tf_op jit(solution)/shard_map/ppermute | solution.py:18
  298.9 5.1 %collective-permute-start.2 = (f32[8,16,6,1]{3,0,2,1:T(8,128)}, f32[8,16,6,1]{3,0,2,1:T(8,128)S(1)}, u32[]{:S(2)}, u32[]{:S(2)}) collective-permute-start(f32[8,16,6,1]{3,0,2,1:T(8,128)} %get-tuple-element.43), channel_id=1, source_target_pairs={{1,0},{2,1},{3,2},{4,3},{5,4},{6,5},{7,6},{8,7},{9,8},{10,9},{11,1... | collective-permute-start | bytes 9224 | tf_op jit(solution)/shard_map/ppermute | solution.py:18
  306.0 6.9 %collective-permute-done.2 = f32[8,16,6,1]{3,0,2,1:T(8,128)S(1)} collective-permute-done((f32[8,16,6,1]{3,0,2,1:T(8,128)}, f32[8,16,6,1]{3,0,2,1:T(8,128)S(1)}, u32[]{:S(2)}, u32[]{:S(2)}) %collective-permute-start.2) | collective-permute-done | bytes 3104 | tf_op jit(solution)/shard_map/ppermute | solution.py:18
  320.7 11.0 %all_to_all.76 = f32[16,2,512]{2,1,0:T(2,128)S(1)} all-to-all(f32[16,2,512]{2,1,0:T(2,128)S(1)} %all_to_all.64), channel_id=1, replica_groups=mesh['wide'=32,'grp'=16] {'grp'}, dimensions={0} | all-to-all | bytes 131072 | tf_op jit(solution)/shard_map/all_to_all | solution.py:74
  331.6 5.6 %rev.14 = f32[2,8192]{1,0:T(2,128)S(1)} reverse(f32[2,8192]{1,0:T(2,128)S(1)} %bitcast.71), dimensions={1} | reverse | bytes 131072 | tf_op jit(solution)/shard_map/rev | solution.py:30
  370.3 5.6 %rev.15 = f32[2,8192]{1,0:T(2,128)S(1)} reverse(f32[2,8192]{1,0:T(2,128)S(1)} %add.491), dimensions={1} | reverse | bytes 131072 | tf_op jit(solution)/shard_map/rev | solution.py:78
  375.8 9.6 %all_to_all.77 = f32[2,16,512]{2,0,1:T(2,128)S(1)} all-to-all(f32[2,16,512]{2,0,1:T(2,128)S(1)} %bitcast.72), channel_id=1, replica_groups=mesh['wide'=32,'grp'=16] {'grp'}, dimensions={1} | all-to-all | bytes 131072 | tf_op jit(solution)/shard_map/all_to_all | solution.py:79
  387.1 8.9 %collective-permute-start.5 = (f32[8,16,1,512]{3,0,2,1:T(8,128)S(1)}, f32[8,16,1,512]{3,0,2,1:T(8,128)S(1)}, u32[]{:S(2)}, u32[]{:S(2)}) collective-permute-start(f32[8,16,1,512]{3,0,2,1:T(8,128)S(1)} %get-tuple-element.45), channel_id=1, source_target_pairs={{0,16},{16,32},{32,48},{48,64},{64,80},{80,96},{96,112},{112,128},... | collective-permute-start | bytes 786440 | tf_op jit(solution)/shard_map/ppermute | solution.py:17
  397.9 10.6 %collective-permute-done.5 = f32[8,16,1,512]{3,0,2,1:T(8,128)S(1)} collective-permute-done((f32[8,16,1,512]{3,0,2,1:T(8,128)S(1)}, f32[8,16,1,512]{3,0,2,1:T(8,128)S(1)}, u32[]{:S(2)}, u32[]{:S(2)}) %collective-permute-start.5) | collective-permute-done | bytes 262176 | tf_op jit(solution)/shard_map/ppermute | solution.py:17
  412.3 5.2 %collective-permute-start.6 = (f32[8,16,6,1]{3,0,2,1:T(8,128)}, f32[8,16,6,1]{3,0,2,1:T(8,128)}, u32[]{:S(2)}, u32[]{:S(2)}) collective-permute-start(f32[8,16,6,1]{3,0,2,1:T(8,128)} %get-tuple-element.41), channel_id=1, source_target_pairs={{1,0},{2,1},{3,2},{4,3},{5,4},{6,5},{7,6},{8,7},{9,8},{10,9},{11,1... | collective-permute-start | bytes 9224 | tf_op jit(solution)/shard_map/ppermute | solution.py:18
  420.1 5.0 %collective-permute-done.6 = f32[8,16,6,1]{3,0,2,1:T(8,128)} collective-permute-done((f32[8,16,6,1]{3,0,2,1:T(8,128)}, f32[8,16,6,1]{3,0,2,1:T(8,128)}, u32[]{:S(2)}, u32[]{:S(2)}) %collective-permute-start.6) | collective-permute-done | bytes 3104 | tf_op jit(solution)/shard_map/ppermute | solution.py:18
  425.1 6.1 %collective-permute-done.7 = f32[8,16,6,1]{3,0,2,1:T(8,128)} collective-permute-done((f32[8,16,6,1]{3,0,2,1:T(8,128)}, f32[8,16,6,1]{3,0,2,1:T(8,128)}, u32[]{:S(2)}, u32[]{:S(2)}) %collective-permute-start.7) | collective-permute-done | bytes 3104 | tf_op jit(solution)/shard_map/ppermute | solution.py:17
  (416 shorter events, 98.3 us)
Async XLA Ops:
  0.6 195.2 %copy-start = (f32[8,8]{1,0:T(8,128)S(1)}, f32[8,8]{1,0:T(8,128)}, u32[]{:S(2)}) copy-start(f32[8,8]{1,0:T(8,128)} %param.22) | copy-start | bytes 772
  1.9 170.1 %all-to-all-start = ((f32[32,1,128]{2,1,0:T(1,128)}), f32[32,1,128]{2,1,0:T(1,128)S(1)}, u32[]{:S(2)}, u32[]{:S(2)}) async-start(f32[32,1,128]{2,1,0:T(1,128)} %stack.2), calls=%async_computation | async-start | bytes 32768 | tf_op jit(solution)/shard_map/all_to_all | solution.py:53
  119.8 95.5 %copy-start.44 = (f32[2]{0:T(128)}, f32[2]{0:T(128)S(1)}, u32[]{:S(2)}) copy-start(f32[2]{0:T(128)S(1)} %get-tuple-element.65) | copy-start | bytes 28
  119.8 108.0 %copy-start.46 = (f32[2]{0:T(128)}, f32[2]{0:T(128)S(1)}, u32[]{:S(2)}) copy-start(f32[2]{0:T(128)S(1)} %get-tuple-element.37) | copy-start | bytes 28
  119.8 109.8 %copy-start.22 = (f32[2]{0:T(128)}, f32[2]{0:T(128)S(1)}, u32[]{:S(2)}) copy-start(f32[2]{0:T(128)S(1)} %get-tuple-element.38) | copy-start | bytes 28
  119.9 112.9 %copy-start.20 = (f32[2]{0:T(128)}, f32[2]{0:T(128)S(1)}, u32[]{:S(2)}) copy-start(f32[2]{0:T(128)S(1)} %get-tuple-element.39) | copy-start | bytes 28
  119.9 110.2 %copy-start.32 = (f32[2]{0:T(128)}, f32[2]{0:T(128)S(1)}, u32[]{:S(2)}) copy-start(f32[2]{0:T(128)S(1)} %get-tuple-element.68) | copy-start | bytes 28
  119.9 110.7 %copy-start.30 = (f32[2]{0:T(128)}, f32[2]{0:T(128)S(1)}, u32[]{:S(2)}) copy-start(f32[2]{0:T(128)S(1)} %get-tuple-element.66) | copy-start | bytes 28
  119.9 111.6 %copy-start.40 = (f32[2]{0:T(128)}, f32[2]{0:T(128)S(1)}, u32[]{:S(2)}) copy-start(f32[2]{0:T(128)S(1)} %get-tuple-element.67) | copy-start | bytes 28
  119.9 114.2 %copy-start.28 = (f32[2]{0:T(128)}, f32[2]{0:T(128)S(1)}, u32[]{:S(2)}) copy-start(f32[2]{0:T(128)S(1)} %get-tuple-element.61) | copy-start | bytes 28
  119.9 115.9 %copy-start.26 = (f32[2]{0:T(128)}, f32[2]{0:T(128)S(1)}, u32[]{:S(2)}) copy-start(f32[2]{0:T(128)S(1)} %get-tuple-element.62) | copy-start | bytes 28
  196.8 12.9 %all-to-all-start.1 = ((f32[16,2,512]{2,1,0:T(2,128)}), f32[16,2,512]{2,1,0:T(2,128)S(1)}, u32[]{:S(2)}, u32[]{:S(2)}) async-start(f32[16,2,512]{2,1,0:T(2,128)} %all_to_all.57), calls=%async_computation.1 | async-start | bytes 131072 | tf_op jit(solution)/shard_map/all_to_all | solution.py:74
  203.9 25.0 %copy-start.36 = (f32[2]{0:T(128)}, f32[2]{0:T(128)S(1)}, u32[]{:S(2)}) copy-start(f32[2]{0:T(128)S(1)} %get-tuple-element.63) | copy-start | bytes 28
  203.9 25.3 %copy-start.34 = (f32[2]{0:T(128)}, f32[2]{0:T(128)S(1)}, u32[]{:S(2)}) copy-start(f32[2]{0:T(128)S(1)} %get-tuple-element.58) | copy-start | bytes 28
  204.9 69.1 %copy-start.24 = (f32[8]{0:T(128)}, f32[8]{0:T(128)S(1)}, u32[]{:S(2)}) copy-start(f32[8]{0:T(128)S(1)} %select_reduce_fusion) | copy-start | bytes 100
  263.3 10.5 %all-to-all-start.2 = ((f32[2,16,512]{2,0,1:T(2,128)}), f32[2,16,512]{2,0,1:T(2,128)S(1)}, u32[]{:S(2)}, u32[]{:S(2)}) async-start(f32[2,16,512]{2,0,1:T(2,128)} %bitcast.21), calls=%async_computation.2 | async-start | bytes 131072 | tf_op jit(solution)/shard_map/all_to_all | solution.py:79
  275.5 8.1 %collective-permute-start.1 = (f32[8,16,1,512]{3,0,2,1:T(8,128)S(1)}, f32[8,16,1,512]{3,0,2,1:T(8,128)S(1)}, u32[]{:S(2)}, u32[]{:S(2)}) collective-permute-start(f32[8,16,1,512]{3,0,2,1:T(8,128)S(1)} %get-tuple-element.47), channel_id=1, source_target_pairs={{0,16},{16,32},{32,48},{48,64},{64,80},{80,96},{96,112},{112,128},... | collective-permute-start | bytes 786440 | tf_op jit(solution)/shard_map/ppermute | solution.py:17
  280.4 17.7 %collective-permute-start = (f32[8,16,1,512]{3,0,2,1:T(8,128)S(1)}, f32[8,16,1,512]{3,0,2,1:T(8,128)S(1)}, u32[]{:S(2)}, u32[]{:S(2)}) collective-permute-start(f32[8,16,1,512]{3,0,2,1:T(8,128)S(1)} %get-tuple-element.48), channel_id=1, source_target_pairs={{16,0},{32,16},{48,32},{64,48},{80,64},{96,80},{112,96},{128,112},... | collective-permute-start | bytes 786440 | tf_op jit(solution)/shard_map/ppermute | solution.py:18
  298.9 14.0 %collective-permute-start.2 = (f32[8,16,6,1]{3,0,2,1:T(8,128)}, f32[8,16,6,1]{3,0,2,1:T(8,128)S(1)}, u32[]{:S(2)}, u32[]{:S(2)}) collective-permute-start(f32[8,16,6,1]{3,0,2,1:T(8,128)} %get-tuple-element.43), channel_id=1, source_target_pairs={{1,0},{2,1},{3,2},{4,3},{5,4},{6,5},{7,6},{8,7},{9,8},{10,9},{11,1... | collective-permute-start | bytes 9224 | tf_op jit(solution)/shard_map/ppermute | solution.py:18
  304.0 14.0 %collective-permute-start.3 = (f32[8,16,6,1]{3,0,2,1:T(8,128)S(1)}, f32[8,16,6,1]{3,0,2,1:T(8,128)}, u32[]{:S(2)}, u32[]{:S(2)}) collective-permute-start(f32[8,16,6,1]{3,0,2,1:T(8,128)S(1)} %get-tuple-element.44), channel_id=1, source_target_pairs={{0,1},{1,2},{2,3},{3,4},{4,5},{5,6},{6,7},{7,8},{8,9},{9,10},{10,1... | collective-permute-start | bytes 9224 | tf_op jit(solution)/shard_map/ppermute | solution.py:17
  387.1 21.4 %collective-permute-start.5 = (f32[8,16,1,512]{3,0,2,1:T(8,128)S(1)}, f32[8,16,1,512]{3,0,2,1:T(8,128)S(1)}, u32[]{:S(2)}, u32[]{:S(2)}) collective-permute-start(f32[8,16,1,512]{3,0,2,1:T(8,128)S(1)} %get-tuple-element.45), channel_id=1, source_target_pairs={{0,16},{16,32},{32,48},{48,64},{64,80},{80,96},{96,112},{112,128},... | collective-permute-start | bytes 786440 | tf_op jit(solution)/shard_map/ppermute | solution.py:17
  396.0 15.3 %collective-permute-start.4 = (f32[8,16,1,512]{3,0,2,1:T(8,128)S(1)}, f32[8,16,1,512]{3,0,2,1:T(8,128)S(1)}, u32[]{:S(2)}, u32[]{:S(2)}) collective-permute-start(f32[8,16,1,512]{3,0,2,1:T(8,128)S(1)} %get-tuple-element.46), channel_id=1, source_target_pairs={{16,0},{32,16},{48,32},{64,48},{80,64},{96,80},{112,96},{128,112},... | collective-permute-start | bytes 786440 | tf_op jit(solution)/shard_map/ppermute | solution.py:18
  412.3 12.8 %collective-permute-start.6 = (f32[8,16,6,1]{3,0,2,1:T(8,128)}, f32[8,16,6,1]{3,0,2,1:T(8,128)}, u32[]{:S(2)}, u32[]{:S(2)}) collective-permute-start(f32[8,16,6,1]{3,0,2,1:T(8,128)} %get-tuple-element.41), channel_id=1, source_target_pairs={{1,0},{2,1},{3,2},{4,3},{5,4},{6,5},{7,6},{8,7},{9,8},{10,9},{11,1... | collective-permute-start | bytes 9224 | tf_op jit(solution)/shard_map/ppermute | solution.py:18
  417.5 13.8 %collective-permute-start.7 = (f32[8,16,6,1]{3,0,2,1:T(8,128)}, f32[8,16,6,1]{3,0,2,1:T(8,128)}, u32[]{:S(2)}, u32[]{:S(2)}) collective-permute-start(f32[8,16,6,1]{3,0,2,1:T(8,128)} %get-tuple-element.42), channel_id=1, source_target_pairs={{0,1},{1,2},{2,3},{3,4},{4,5},{5,6},{6,7},{7,8},{8,9},{9,10},{10,1... | collective-permute-start | bytes 9224 | tf_op jit(solution)/shard_map/ppermute | solution.py:17
  (60 other events, 140.8 us)
